TPU v7x, 32 devices: a whole 2x2x4 slice. The times are simulated.
32 devices in a mesh: pipe: 2 (over x), expert: 16 (over z, y, core).
Axes of the slice: x: 2, y: 2, z: 4, core: 2. Of those that a mesh axis runs over, the one named last changes fastest.
Arguments:
- tokens: bfloat16 [2048, 1024], P('expert'), may hold values from -6 to 6
- out_grad: bfloat16 [2048, 1024], P('expert'), may hold values from -6 to 6
- routes: int32 [2048, 6], P('expert'), may hold values from 0 to 15, as said below
- slots: int32 [2048, 6], P('expert'), may hold values from 0 to 63, as said below
- gates: bfloat16 [2048, 6], P('expert'), may hold values from 0.099609375 to 1
- w_gate: bfloat16 [16, 1408, 1024], P('expert', 'pipe'), may hold values from -0.1875 to 0.1875
- w_up: bfloat16 [16, 1408, 1024], P('expert', 'pipe'), may hold values from -0.1875 to 0.1875
- w_down: bfloat16 [16, 1408, 1024], P('expert', 'pipe'), may hold values from -0.15625 to 0.15625
Outputs:
- mixed: bfloat16 [2048, 1024], P('expert', 'pipe')
- grad_tokens: bfloat16 [2048, 1024], P('expert', 'pipe')
- grad_gates: float32 [2048, 6], P('expert')
- grad_w_gate: bfloat16 [16, 1408, 1024], P('expert', 'pipe')
- grad_w_up: bfloat16 [16, 1408, 1024], P('expert', 'pipe')
- grad_w_down: bfloat16 [16, 1408, 1024], P('expert', 'pipe')
Inputs may be any that keep to these rules, and one draw needn't show every extreme that they name: `routes`: each token names 6 different experts. Within one device's block of 128 tokens no expert is named more than 64 times, and some expert is named exactly 64 times by every block. Within one block of 128 tokens the pairs (routes, slots) are all different.
All inputs are finite; a program needn't handle non-finite values.
Results may differ from a plain program's by a relative error of at most 0.015.
Values may be sent and summed in bfloat16 or wider, within the bound.
A program may use at most 64 MiB of HBM per device.

v0:
```python
import jax
import jax.numpy as jnp
from jax import lax
from jax.sharding import PartitionSpec as P


def expert_forward(arrived_x, gate_w, up_w, down_w):
    contract = (((1,), (1,)), ((), ()))
    gate_pre = lax.dot_general(arrived_x, gate_w, contract, preferred_element_type=jnp.float32)
    up_pre = lax.dot_general(arrived_x, up_w, contract, preferred_element_type=jnp.float32)
    sigma = jax.nn.sigmoid(gate_pre)
    silu_val = gate_pre * sigma
    act = (silu_val * up_pre).astype(jnp.bfloat16)
    partial_out = jnp.dot(act, down_w, preferred_element_type=jnp.float32).astype(jnp.bfloat16)
    return (partial_out, (gate_pre, up_pre, sigma, silu_val, act))


def expert_backward(arrived_x, arrived_dy, arrived_g, saved, gate_w, up_w, down_w):
    gate_pre, up_pre, sigma, silu_val, act = saved
    contract = (((1,), (1,)), ((), ()))
    over_rows = (((0,), (0,)), ((), ()))
    d_out = (arrived_g.astype(jnp.float32)[:, None] * arrived_dy.astype(jnp.float32)).astype(
        jnp.bfloat16
    )
    d_act = lax.dot_general(d_out, down_w, contract, preferred_element_type=jnp.float32)
    d_gate = (d_act * up_pre * sigma * (1.0 + gate_pre * (1.0 - sigma))).astype(jnp.bfloat16)
    d_up = (d_act * silu_val).astype(jnp.bfloat16)
    partial_back = (
        jnp.dot(d_gate, gate_w, preferred_element_type=jnp.float32)
        + jnp.dot(d_up, up_w, preferred_element_type=jnp.float32)
    ).astype(jnp.bfloat16)
    grad_gate_w = lax.dot_general(
        d_gate, arrived_x, over_rows, preferred_element_type=jnp.float32
    ).astype(jnp.bfloat16)
    grad_up_w = lax.dot_general(
        d_up, arrived_x, over_rows, preferred_element_type=jnp.float32
    ).astype(jnp.bfloat16)
    grad_down_w = lax.dot_general(act, d_out, over_rows, preferred_element_type=jnp.float32).astype(
        jnp.bfloat16
    )
    return (partial_back, (grad_gate_w[None], grad_up_w[None], grad_down_w[None]))


def pick_rows(returned, flat_slot, local_tokens, topk):
    slot_total = returned.shape[0] * returned.shape[1]
    flat_back = returned.reshape(slot_total, returned.shape[2])
    return jnp.take(flat_back, flat_slot, axis=0).reshape(local_tokens, topk, returned.shape[2])


def body(tokens, out_grad, routes, slots, gates, w_gate, w_up, w_down):
    local_tokens = tokens.shape[0]
    topk = routes.shape[1]
    sources = lax.axis_size("expert")
    experts = sources * w_gate.shape[0]
    capacity = 4 * local_tokens * topk // (3 * experts)
    slot_total = experts * capacity
    flat_slot = (routes * capacity + slots).reshape(-1)
    owner_token = jnp.arange(local_tokens * topk, dtype=jnp.int32) // topk
    owner = jnp.full((slot_total,), local_tokens, jnp.int32).at[flat_slot].set(owner_token)
    gate_slot = (
        jnp.zeros((slot_total,), jnp.bfloat16)
        .at[flat_slot]
        .set(gates.reshape(-1))
        .reshape(experts, capacity)
    )
    share = tokens.shape[1] // lax.axis_size("pipe")
    begin = lax.axis_index("pipe") * share

    def fill_rows(matrix):
        taken = jnp.take(matrix, owner, axis=0, mode="fill", fill_value=0)
        return taken.reshape(experts, capacity, matrix.shape[1])

    x_share = lax.dynamic_slice_in_dim(tokens, begin, share, 1)
    dy_share = lax.dynamic_slice_in_dim(out_grad, begin, share, 1)
    part_x, part_dy, arrived_g = (
        lax.all_to_all(fill_rows(x_share), "expert", split_axis=0, concat_axis=0, tiled=True),
        lax.all_to_all(fill_rows(dy_share), "expert", split_axis=0, concat_axis=0, tiled=True),
        lax.all_to_all(gate_slot, "expert", split_axis=0, concat_axis=0, tiled=True),
    )
    arrived_x, arrived_dy = (
        lax.all_gather(part_x, "pipe", axis=2, tiled=True),
        lax.all_gather(part_dy, "pipe", axis=2, tiled=True),
    )
    row_count = sources * capacity
    width = arrived_x.shape[2]
    arrived_x = arrived_x.reshape(row_count, width)
    arrived_dy = arrived_dy.reshape(row_count, width)
    arrived_g = arrived_g.reshape(row_count)
    gate_w = w_gate[0]
    up_w = w_up[0]
    down_w = w_down[0]
    ones_weight = jnp.ones((local_tokens, topk), jnp.bfloat16)
    batch_k = (((1,), (1,)), ((0,), (0,)))
    batch_d = (((2,), (1,)), ((0,), (0,)))
    partial_out, saved = expert_forward(arrived_x, gate_w, up_w, down_w)
    out_back = lax.all_to_all(
        partial_out.reshape(sources, capacity, width),
        "expert",
        split_axis=0,
        concat_axis=0,
        tiled=True,
    )
    picked = pick_rows(out_back, flat_slot, local_tokens, topk)
    mixed_part = lax.dot_general(gates, picked, batch_k, preferred_element_type=jnp.float32)
    gate_part = lax.dot_general(picked, out_grad, batch_d, preferred_element_type=jnp.float32)
    mixed_sum = lax.psum_scatter(
        mixed_part.astype(jnp.bfloat16), "pipe", scatter_dimension=1, tiled=True
    )
    partial_back, weight_grads = expert_backward(
        arrived_x, arrived_dy, arrived_g, saved, gate_w, up_w, down_w
    )
    grad_back = lax.all_to_all(
        partial_back.reshape(sources, capacity, width),
        "expert",
        split_axis=0,
        concat_axis=0,
        tiled=True,
    )
    picked_grad = pick_rows(grad_back, flat_slot, local_tokens, topk)
    grad_part = lax.dot_general(
        ones_weight, picked_grad, batch_k, preferred_element_type=jnp.float32
    )
    grad_total = lax.psum_scatter(
        grad_part.astype(jnp.bfloat16), "pipe", scatter_dimension=1, tiled=True
    )
    grad_gates = lax.psum(gate_part, "pipe")
    return (mixed_sum, grad_total, grad_gates, weight_grads[0], weight_grads[1], weight_grads[2])


def solution(mesh):
    return jax.shard_map(
        body,
        mesh=mesh,
        in_specs=(
            P("expert", None),
            P("expert", None),
            P("expert", None),
            P("expert", None),
            P("expert", None),
            P("expert", "pipe", None),
            P("expert", "pipe", None),
            P("expert", "pipe", None),
        ),
        out_specs=(
            P("expert", "pipe"),
            P("expert", "pipe"),
            P("expert", None),
            P("expert", "pipe", None),
            P("expert", "pipe", None),
            P("expert", "pipe", None),
        ),
        check_vma=False,
    )
```

profile of v0, /device:TPU:0, one launch (start us, length us, event | category | flops | bytes accessed | tf_op | source)
XLA Modules:
  0.0 287.2 jit_solution(10772181095873960082)
XLA Ops:
  7.2 0.8 multiply_add_fusion
  8.2 0.1 reshape.110
  8.3 3.4 %scatter_custom_fusion = s32[1024]{0:T(1024)S(1)} fusion(s32[768]{0:T(1024)S(1)} %fusion.23, s32[768]{0:T(1024)S(1)} %add_select_fusion, s32[]{:T(128)} %constant.34.clone.1), kind=kCustom, calls=%fused_computation.58 | custom fusion | bytes 4100 | tf_op jit(solution)/shard_map/scatter | solution.py:59
  11.8 1.0 constant_dynamic-slice_fusion
  12.8 4.0 %gather_fusion.2 = bf16[1024,512]{1,0:T(8,128)(2,1)S(1)} fusion(bf16[128,512]{1,0:T(8,128)(2,1)S(1)} %get-tuple-element.15, s32[1024]{0:T(1024)S(1)} %fusion.22), kind=kCustom, calls=%fused_computation.2.clone | custom fusion | bytes 2101248 | tf_op jit(solution)/shard_map/jit(_take)/gather | solution.py:70
  16.7 5.1 %gather_fusion = bf16[1024,512]{1,0:T(8,128)(2,1)} fusion(bf16[128,512]{1,0:T(8,128)(2,1)S(1)} %get-tuple-element.16, s32[1024]{0:T(1024)S(1)} %fusion.22), kind=kCustom, calls=%fused_computation.clone | custom fusion | bytes 2101248 | tf_op jit(solution)/shard_map/jit(_take)/gather | solution.py:70
  21.8 2.4 broadcast_select_fusion.2
  24.2 32.1 %all_to_all.30 = bf16[16,64,512]{2,1,0:T(8,128)(2,1)} all-to-all(bf16[16,64,512]{2,1,0:T(8,128)(2,1)S(1)} %bitcast.65), channel_id=1, replica_groups=mesh['pipe'=2,'expert'=16] {'expert'}, dimensions={0} | all-to-all | bytes 2097152 | tf_op jit(solution)/shard_map/all_to_all | solution.py:76
  56.4 29.6 %all_to_all.31 = bf16[16,64,512]{2,1,0:T(8,128)(2,1)} all-to-all(bf16[16,64,512]{2,1,0:T(8,128)(2,1)S(1)} %bitcast.64), channel_id=1, replica_groups=mesh['pipe'=2,'expert'=16] {'expert'}, dimensions={0} | all-to-all | bytes 2097152 | tf_op jit(solution)/shard_map/all_to_all | solution.py:77
  86.2 0.2 reshape.169
  86.4 8.6 %scatter_custom_fusion.1 = bf16[1024]{0:T(1024)(128)(2,1)S(1)} fusion(s32[768]{0:T(1024)S(1)} %fusion.23, bf16[768]{0:T(1024)(128)(2,1)S(1)} %reshape.169, bf16[]{:T(256)} %constant.22.clone.1), kind=kCustom, calls=%fused_computation.60 | custom fusion | bytes 2050 | tf_op jit(solution)/shard_map/scatter | solution.py:63
  95.1 11.2 %all_to_all.32 = bf16[16,1,64]{2,1,0:T(2,128)(2,1)S(1)} all-to-all(bf16[16,1,64]{2,1,0:T(2,128)(2,1)S(1)} %all_to_all.24), channel_id=1, replica_groups=mesh['pipe'=2,'expert'=16] {'expert'}, dimensions={0} | all-to-all | bytes 4096 | tf_op jit(solution)/shard_map/all_to_all | solution.py:78
  106.4 5.4 %fusion.9 = f32[1024,704]{0,1:T(8,128)} fusion(bf16[1024,1024]{1,0:T(8,128)(2,1)} %bitcast.75, bf16[1,704,1024]{2,1,0:T(8,128)(2,1)} %param.18), kind=kOutput, calls=%fused_computation.28 | convolution fusion | flops 1476395008 | bytes 6422528 | tf_op jit(solution)/shard_map/dot_general | solution.py:10
  111.8 3.3 %fusion.13 = f32[1024,704]{0,1:T(8,128)} fusion(bf16[1024,1024]{1,0:T(8,128)(2,1)S(1)} %bitcast.77, bf16[1,704,1024]{2,1,0:T(8,128)(2,1)S(1)} %copy-done.9), kind=kOutput, calls=%fused_computation.32 | convolution fusion | flops 1476395008 | bytes 6422528 | tf_op jit(solution)/shard_map/dot_general | solution.py:9
  115.1 9.6 %all-gather.5.cloned.1.call-done = bf16[16,64,1024]{2,1,0:T(8,128)(2,1)} async-done(((bf16[16,64,512]{2,1,0:T(8,128)(2,1)}), bf16[16,64,1024]{2,1,0:T(8,128)(2,1)}) %all-gather.5.cloned.1.call-update) | async-done | bytes 2097168 | tf_op jit(solution)/shard_map/all_gather | solution.py:82
  124.7 2.1 multiply_convert_fusion
  126.8 0.3 copy-done.11
  127.1 5.4 %multiply_convert_fusion.1 = (bf16[1024,704]{0,1:T(8,128)(2,1)}, bf16[1024,704]{0,1:T(8,128)(2,1)}, bf16[1024,704]{0,1:T(8,128)(2,1)S(1)}) fusion(f32[1024,704]{0,1:T(8,128)} %fusion.13, f32[1024,704]{0,1:T(8,128)S(1)} %copy-done.11, bf16[1024,1024]{1,0:T(8,128)(2,1)S(1)} %bitcast.68, bf16[1,704,1024]{2,1,0:T(8,128)(2,1)S(1)} %copy-done), kind=kOutput, calls=%fused_computation.10 | convolution fusion | flops 1487208448 | bytes 13631488 | tf_op jit(solution)/shard_map/dot_general | solution.py:25
  132.6 3.2 %convolution_convert_fusion = bf16[1024,1024]{1,0:T(8,128)(2,1)} fusion(bf16[1024,704]{0,1:T(8,128)(2,1)S(1)} %get-tuple-element.10, bf16[1,704,1024]{2,1,0:T(8,128)(2,1)S(1)} %copy-done), kind=kOutput, calls=%fused_computation.15 | convolution fusion | flops 1477443584 | bytes 4980736 | tf_op jit(solution)/shard_map/dot_general | solution.py:14
  135.7 5.6 %all-to-all-start.1 = ((bf16[16,64,1024]{2,1,0:T(8,128)(2,1)}), bf16[16,64,1024]{2,1,0:T(8,128)(2,1)S(1)}, u32[]{:S(2)}, u32[]{:S(2)}) async-start(bf16[16,64,1024]{2,1,0:T(8,128)(2,1)} %bitcast.67), calls=%async_computation.1 | async-start | bytes 4194304 | tf_op jit(solution)/shard_map/all_to_all | solution.py:96
  141.4 3.8 %fusion.11 = f32[1024,1024]{1,0:T(8,128)S(1)} fusion(bf16[1024,704]{0,1:T(8,128)(2,1)} %get-tuple-element.9, bf16[1,704,1024]{2,1,0:T(8,128)(2,1)} %param.17), kind=kOutput, calls=%fused_computation.30 | convolution fusion | flops 1476395008 | bytes 7077888 | tf_op jit(solution)/shard_map/dot_general | solution.py:29
  145.2 3.3 %add_convert_fusion = bf16[1024,1024]{1,0:T(8,128)(2,1)} fusion(f32[1024,1024]{1,0:T(8,128)S(1)} %fusion.11, bf16[1024,704]{0,1:T(8,128)(2,1)S(1)} %copy-done.13, bf16[1,704,1024]{2,1,0:T(8,128)(2,1)S(1)} %copy-done.10), kind=kOutput, calls=%fused_computation.8 | convolution fusion | flops 1478492160 | bytes 9175040 | tf_op jit(solution)/shard_map/dot_general | solution.py:30
  148.5 33.8 %all-to-all-done.1 = bf16[16,64,1024]{2,1,0:T(8,128)(2,1)S(1)} async-done(((bf16[16,64,1024]{2,1,0:T(8,128)(2,1)}), bf16[16,64,1024]{2,1,0:T(8,128)(2,1)S(1)}, u32[]{:S(2)}, u32[]{:S(2)}) %all-to-all-start.1) | async-done | bytes 2097184 | tf_op jit(solution)/shard_map/all_to_all | solution.py:96
  182.3 11.3 %all-to-all-start.4 = ((bf16[16,64,1024]{2,1,0:T(8,128)(2,1)}), bf16[16,64,1024]{2,1,0:T(8,128)(2,1)}, u32[]{:S(2)}, u32[]{:S(2)}) async-start(bf16[16,64,1024]{2,1,0:T(8,128)(2,1)} %bitcast.66), calls=%async_computation.5 | async-start | bytes 4194304 | tf_op jit(solution)/shard_map/all_to_all | solution.py:112
  193.6 0.3 reduce-scatter.5.cloned.1.call-start
  193.9 1.0 reshape.115
  194.9 0.8 copy.24
  195.6 0.6 compare_and_fusion
  196.2 0.6 convert_reduce_fusion
  196.8 0.8 reshape.123
  197.6 4.9 %fusion.3 = bf16[1,704,1024]{2,1,0:T(8,128)(2,1)} fusion(bf16[1024,704]{0,1:T(8,128)(2,1)} %get-tuple-element.8, bf16[1024,1024]{1,0:T(8,128)(2,1)} %bitcast.76), kind=kOutput, calls=%fused_computation.22 | convolution fusion | flops 1477115904 | bytes 4980736 | tf_op jit(solution)/shard_map/dot_general | solution.py:35
  202.5 2.8 fusion.2
  205.3 3.6 %gather_fusion.1 = bf16[768,1024]{1,0:T(8,128)(2,1)} fusion(bf16[1024,1024]{1,0:T(8,128)(2,1)S(1)} %bitcast.63, s32[1024]{0:T(1024)S(1)} %pad_clamp_fusion), kind=kCustom, calls=%fused_computation.1.clone | custom fusion | bytes 3148800 | tf_op jit(solution)/shard_map/jit(_take)/gather | solution.py:47
  208.9 25.7 %all-to-all-done.4 = bf16[16,64,1024]{2,1,0:T(8,128)(2,1)} async-done(((bf16[16,64,1024]{2,1,0:T(8,128)(2,1)}), bf16[16,64,1024]{2,1,0:T(8,128)(2,1)}, u32[]{:S(2)}, u32[]{:S(2)}) %all-to-all-start.4) | async-done | bytes 2097184 | tf_op jit(solution)/shard_map/all_to_all | solution.py:112
  234.7 6.6 %gather_fusion.3 = bf16[768,1024]{1,0:T(8,128)(2,1)} fusion(bf16[1024,1024]{1,0:T(8,128)(2,1)} %bitcast.13, s32[1024]{0:T(1024)S(1)} %pad_clamp_fusion), kind=kCustom, calls=%fused_computation.3.clone | custom fusion | bytes 3148800 | tf_op jit(solution)/shard_map/jit(_take)/gather | solution.py:47
  241.2 3.5 %broadcast_select_fusion = (bf16[768,1024]{1,0:T(8,128)(2,1)}, bf16[768,1024]{1,0:T(8,128)(2,1)}) fusion(bf16[768,1024]{1,0:T(8,128)(2,1)} %gather_fusion.3, pred[768]{0:T(1024)(128)(4,1)S(1)} %copy-done.6, bf16[768,1024]{1,0:T(8,128)(2,1)S(1)} %copy-done.1), kind=kLoop, calls=%fused_computation.19 | loop fusion | flops 1572864 | bytes 6292224 | tf_op jit(solution)/shard_map/jit(_take)/select_n | solution.py:47
  244.7 2.5 reshape.121
  247.2 0.7 fusion.17
  247.9 0.8 copy.34
  248.8 3.3 %fusion = bf16[1024,1024]{1,0:T(8,128)(2,1)} fusion(f32[1024]{0:T(1024)S(1)} %reshape.123, bf16[16,64,1024]{2,1,0:T(8,128)(2,1)} %all-gather.5.cloned.1.call-done), kind=kLoop, calls=%fused_computation.7 | loop fusion | flops 3145728 | bytes 4198400 | tf_op jit(solution)/shard_map/convert_element_type | solution.py:22
  252.1 2.5 reshape.116
  254.6 1.5 fusion.29
  256.1 0.8 copy.35
  257.0 4.8 %fusion.4 = bf16[1,704,1024]{2,1,0:T(8,128)(2,1)} fusion(bf16[1024,704]{0,1:T(8,128)(2,1)} %copy-done.14, bf16[1024,1024]{1,0:T(8,128)(2,1)} %fusion), kind=kOutput, calls=%fused_computation.23 | convolution fusion | flops 1477115904 | bytes 4980736 | tf_op jit(solution)/shard_map/dot_general | solution.py:38
  261.8 2.1 fusion.15
  263.8 0.9 copy.29
  264.7 5.5 %psum.7 = f32[128,6]{0,1:T(8,128)} all-reduce(f32[128,6]{0,1:T(8,128)S(1)} %bitcast.73), channel_id=1, replica_groups=mesh['pipe'=2,'expert'=16] {'pipe'}, use_global_device_ids=true, to_apply=%region_4.7 | all-reduce | flops 768 | bytes 6144 | tf_op jit(solution)/shard_map/psum | solution.py:126
  270.3 10.4 %reduce-scatter.3.cloned.1.call-done = bf16[128,512]{1,0:T(8,128)(2,1)} async-done(((bf16[128,1024]{1,0:T(8,128)(2,1)}), bf16[128,512]{1,0:T(8,128)(2,1)}) %reduce-scatter.3.cloned.1.call-update) | async-done | bytes 131088 | tf_op jit(solution)/shard_map/reduce_scatter | solution.py:106
  (48 shorter events, 0.7 us)
Async XLA Ops:
  7.2 119.7 %copy-start = (bf16[1,704,1024]{2,1,0:T(8,128)(2,1)S(1)}, bf16[1,704,1024]{2,1,0:T(8,128)(2,1)}, u32[]{:S(2)}) copy-start(bf16[1,704,1024]{2,1,0:T(8,128)(2,1)} %param.19) | copy-start | bytes 4325380
  7.2 99.2 %all-gather.3.cloned.1.call-start = ((), (), s32[]{:S(2)}) async-start(), calls=%async_computation.7 | async-start | bytes 3145728 | tf_op jit(solution)/shard_map/all_gather | solution.py:81
  8.2 3.6 %copy-start.3 = (s32[128,6]{1,0:T(8,128)}, s32[128,6]{1,0:T(8,128)S(1)}, u32[]{:S(2)}) copy-start(s32[128,6]{1,0:T(8,128)S(1)} %copy.20) | copy-start | bytes 9220
  24.2 32.2 %copy-start.2 = (bf16[1024,512]{1,0:T(8,128)(2,1)S(1)}, bf16[1024,512]{1,0:T(8,128)(2,1)}, u32[]{:S(2)}) copy-start(bf16[1024,512]{1,0:T(8,128)(2,1)} %get-tuple-element.13) | copy-start | bytes 3145732
  56.4 29.7 %copy-start.5 = (bf16[128,6]{0,1:T(8,128)(2,1)S(1)}, bf16[128,6]{0,1:T(8,128)(2,1)}, u32[]{:S(2)}) copy-start(bf16[128,6]{0,1:T(8,128)(2,1)} %param.16) | copy-start | bytes 4612
  56.4 68.3 %all-gather.5.cloned.1.call-start = ((), (), s32[]{:S(2)}) async-start(), calls=%async_computation.9 | async-start | bytes 3145728 | tf_op jit(solution)/shard_map/all_gather | solution.py:82
  106.4 5.5 %copy-start.7 = (bf16[16,64,1024]{2,1,0:T(8,128)(2,1)S(1)}, bf16[16,64,1024]{2,1,0:T(8,128)(2,1)}, u32[]{:S(2)}) copy-start(bf16[16,64,1024]{2,1,0:T(8,128)(2,1)} %all-gather.3.cloned.1.call-done) | copy-start | bytes 6291460
  106.4 5.5 %copy-start.9 = (bf16[1,704,1024]{2,1,0:T(8,128)(2,1)S(1)}, bf16[1,704,1024]{2,1,0:T(8,128)(2,1)}, u32[]{:S(2)}) copy-start(bf16[1,704,1024]{2,1,0:T(8,128)(2,1)} %param.17) | copy-start | bytes 4325380
  124.7 2.4 copy-start.11
  132.6 3.2 %copy-start.14 = (bf16[1024,704]{0,1:T(8,128)(2,1)}, bf16[1024,704]{0,1:T(8,128)(2,1)S(1)}, u32[]{:S(2)}) copy-start(bf16[1024,704]{0,1:T(8,128)(2,1)S(1)} %get-tuple-element.10) | copy-start | bytes 4325380
  135.7 46.6 %all-to-all-start.1 = ((bf16[16,64,1024]{2,1,0:T(8,128)(2,1)}), bf16[16,64,1024]{2,1,0:T(8,128)(2,1)S(1)}, u32[]{:S(2)}, u32[]{:S(2)}) async-start(bf16[16,64,1024]{2,1,0:T(8,128)(2,1)} %bitcast.67), calls=%async_computation.1 | async-start | bytes 4194304 | tf_op jit(solution)/shard_map/all_to_all | solution.py:96
  141.4 3.8 %copy-start.10 = (bf16[1,704,1024]{2,1,0:T(8,128)(2,1)S(1)}, bf16[1,704,1024]{2,1,0:T(8,128)(2,1)}, u32[]{:S(2)}) copy-start(bf16[1,704,1024]{2,1,0:T(8,128)(2,1)} %param.18) | copy-start | bytes 4325380
  141.4 3.8 %copy-start.13 = (bf16[1024,704]{0,1:T(8,128)(2,1)S(1)}, bf16[1024,704]{0,1:T(8,128)(2,1)}, u32[]{:S(2)}) copy-start(bf16[1024,704]{0,1:T(8,128)(2,1)} %get-tuple-element.8) | copy-start | bytes 4325380
  182.3 52.3 %all-to-all-start.4 = ((bf16[16,64,1024]{2,1,0:T(8,128)(2,1)}), bf16[16,64,1024]{2,1,0:T(8,128)(2,1)}, u32[]{:S(2)}, u32[]{:S(2)}) async-start(bf16[16,64,1024]{2,1,0:T(8,128)(2,1)} %bitcast.66), calls=%async_computation.5 | async-start | bytes 4194304 | tf_op jit(solution)/shard_map/all_to_all | solution.py:112
  193.6 76.7 %reduce-scatter.5.cloned.1.call-start = ((), (), s32[]{:S(2)}) async-start(), calls=%async_computation.10 | async-start | bytes 393216 | tf_op jit(solution)/shard_map/reduce_scatter | solution.py:123
  197.6 4.9 %copy-start.8 = (bf16[16,64,1024]{2,1,0:T(8,128)(2,1)S(1)}, bf16[16,64,1024]{2,1,0:T(8,128)(2,1)}, u32[]{:S(2)}) copy-start(bf16[16,64,1024]{2,1,0:T(8,128)(2,1)} %all-gather.3.cloned.1.call-done) | copy-start | bytes 6291460
  197.6 4.9 %copy-start.12 = (bf16[1024,704]{0,1:T(8,128)(2,1)S(1)}, bf16[1024,704]{0,1:T(8,128)(2,1)}, u32[]{:S(2)}) copy-start(bf16[1024,704]{0,1:T(8,128)(2,1)} %get-tuple-element.9) | copy-start | bytes 4325380
  234.6 6.6 %copy-start.1 = (bf16[768,1024]{1,0:T(8,128)(2,1)S(1)}, bf16[768,1024]{1,0:T(8,128)(2,1)}, u32[]{:S(2)}) copy-start(bf16[768,1024]{1,0:T(8,128)(2,1)} %gather_fusion.1) | copy-start | bytes 4718596
  234.6 6.6 %copy-start.6 = (pred[768]{0:T(1024)(128)(4,1)S(1)}, pred[768]{0:T(1024)(128)(4,1)}, u32[]{:S(2)}) copy-start(pred[768]{0:T(1024)(128)(4,1)} %compare_and_fusion) | copy-start | bytes 2308
  248.7 32.0 %reduce-scatter.3.cloned.1.call-start = ((), (), s32[]{:S(2)}) async-start(), calls=%async_computation.8 | async-start | bytes 393216 | tf_op jit(solution)/shard_map/reduce_scatter | solution.py:106
  256.9 4.8 %copy-start.4 = (bf16[128,1024]{1,0:T(8,128)(2,1)S(1)}, bf16[128,1024]{1,0:T(8,128)(2,1)}, u32[]{:S(2)}) copy-start(bf16[128,1024]{1,0:T(8,128)(2,1)} %param.13) | copy-start | bytes 786436
Sparse Core Ops, SparseCore 0:
  56.5 33.4 all-gather.2
  91.6 33.0 all-gather.4
  248.8 17.3 reduce-scatter.4
  268.9 11.7 reduce-scatter.2
where the time goes:
time: 288 us; the launch traced here: 287 us
  waiting for transfers between devices  79.6 us (28%)
  blocking collectives  78.5 us (27%)
  local copies, waits for them, and re-layouts  43.1 us (15%)
  matrix products  41.2 us (14%)
  starting transfers between devices  17.3 us (6%)
  between operations  14 us (5%)
  other arithmetic  13.5 us (5%)
    all_to_all x1, waiting for transfers between devices, body(): lax.all_to_all(partial_out.reshape(sources, capacity, width), 'expert', s...  33.8 us
    all_to_all x1, blocking collectives, body(): lax.all_to_all(fill_rows(x_share), 'expert', split_axis=0, concat_axis=0,...  32.1 us
    all_to_all x1, blocking collectives, body(): lax.all_to_all(fill_rows(dy_share), 'expert', split_axis=0, concat_axis=0...  29.6 us
    all_to_all x1, waiting for transfers between devices, body(): lax.all_to_all(partial_back.reshape(sources, capacity, width), 'expert',...  25.7 us
    all_to_all x1, starting transfers between devices, body(): lax.all_to_all(partial_back.reshape(sources, capacity, width), 'expert',...  11.3 us
    all_to_all x1, blocking collectives, body(): lax.all_to_all(gate_slot, 'expert', split_axis=0, concat_axis=0, tiled=True)  11.2 us
    reduce_scatter x1, waiting for transfers between devices, body(): lax.psum_scatter(mixed_part.astype(jnp.bfloat16), 'pipe', scatter_dimensi...  10.4 us
    gather x2, local copies, waits for them, and re-layouts, pick_rows(): jnp.take(flat_back, flat_slot, axis=0)  10.1 us
  transfers between devices with their start and end apart: 6, of which 4 were waited for; matrix products, arithmetic and copies ran while one was open for 19% of the time, Pallas kernels for 0%

commit v1 on v0

--- a/solution.py
+++ b/solution.py
@@ -1,7 +1,40 @@
+import functools
 import jax
 import jax.numpy as jnp
 from jax import lax
 from jax.sharding import PartitionSpec as P
+
+
+def draw_steps_all(buf, dim_k, block_here):
+    before, later = (buf.shape[:dim_k], buf.shape[dim_k + 1 :])
+    new = jnp.moveaxis(buf.reshape(*before, block_here, -1, *later), dim_k, 0)
+    return new
+
+
+def press_lines(w_in, along_dim):
+    main = list(w_in.shape[1:])
+    main[along_dim] *= w_in.shape[0]
+    mat_out = jnp.moveaxis(w_in, 0, along_dim).reshape(main)
+    return mat_out
+
+
+def drive_floor_on(array_here, link_axis, view, vals):
+    low, next_value = (jax.lax.axis_size(link_axis), jax.lax.axis_index(link_axis))
+    reply = draw_steps_all(array_here, view, low)
+    seen = [reply[next_value]]
+    for d in range(1, low):
+        field_out = reply[(next_value + d) % low]
+        seen.append(
+            jax.lax.ppermute(
+                field_out, axis_name=link_axis, perm=[(m, (m + d) % low) for m in range(low)]
+            )
+        )
+    reply = jnp.stack(seen)[(next_value - jnp.arange(low)) % low]
+    current_block = press_lines(reply, vals)
+    return current_block
+
+
+record_choose = functools.partial(drive_floor_on, link_axis="expert", view=0, vals=0)
 
 
 def expert_forward(arrived_x, gate_w, up_w, down_w):
@@ -73,7 +106,7 @@
     x_share = lax.dynamic_slice_in_dim(tokens, begin, share, 1)
     dy_share = lax.dynamic_slice_in_dim(out_grad, begin, share, 1)
     part_x, part_dy, arrived_g = (
-        lax.all_to_all(fill_rows(x_share), "expert", split_axis=0, concat_axis=0, tiled=True),
+        record_choose(fill_rows(x_share)),
         lax.all_to_all(fill_rows(dy_share), "expert", split_axis=0, concat_axis=0, tiled=True),
         lax.all_to_all(gate_slot, "expert", split_axis=0, concat_axis=0, tiled=True),
     )

time: 288 us -> 327 us (1.14)
  waiting for transfers between devices: 79.6 us -> 136 us
  blocking collectives: 78.5 us -> 49.5 us
  starting transfers between devices: 17.3 us -> 27.7 us
    ppermute x0 -> x15, waiting for transfers between devices: none -> 55.9 us  [drive_floor_on(): jax.lax.ppermute(field_out, axis_name=link_axis, perm=[(m, (m + d) % low)...]
    all_to_all x1 -> x0, blocking collectives: 32.1 us -> none  [body(): lax.all_to_all(fill_rows(x_share), 'expert', split_axis=0, concat_axis=0,...]
    ppermute x0 -> x15, starting transfers between devices: none -> 10.4 us  [drive_floor_on(): jax.lax.ppermute(field_out, axis_name=link_axis, perm=[(m, (m + d) % low)...]
  transfers between devices with their start and end apart: 6 -> 21, of which waited for: 4 -> 15; matrix products, arithmetic and copies ran while one was open for 19% -> 17% of each run, Pallas kernels for 0% -> 0%
where the time goes in v1:
time: 327 us
  waiting for transfers between devices  136 us (42%)
  blocking collectives  49.5 us (15%)
  local copies, waits for them, and re-layouts  44.8 us (14%)
  matrix products  41.2 us (13%)
  starting transfers between devices  27.7 us (8%)
  between operations  14.3 us (4%)
  other arithmetic  13.5 us (4%)
    ppermute x15, waiting for transfers between devices, drive_floor_on(): jax.lax.ppermute(field_out, axis_name=link_axis, perm=[(m, (m + d) % low)...  55.9 us
    all_to_all x1, waiting for transfers between devices, body(): lax.all_to_all(partial_out.reshape(sources, capacity, width), 'expert', s...  33.8 us
    all_to_all x1, blocking collectives, body(): lax.all_to_all(fill_rows(dy_share), 'expert', split_axis=0, concat_axis=0...  32.7 us
    all_to_all x1, waiting for transfers between devices, body(): lax.all_to_all(partial_back.reshape(sources, capacity, width), 'expert',...  25.8 us
    all_to_all x1, starting transfers between devices, body(): lax.all_to_all(partial_back.reshape(sources, capacity, width), 'expert',...  11.3 us
    all_to_all x1, blocking collectives, body(): lax.all_to_all(gate_slot, 'expert', split_axis=0, concat_axis=0, tiled=True)  11.2 us
    ppermute x15, starting transfers between devices, drive_floor_on(): jax.lax.ppermute(field_out, axis_name=link_axis, perm=[(m, (m + d) % low)...  10.4 us
    reduce_scatter x1, waiting for transfers between devices, body(): lax.psum_scatter(mixed_part.astype(jnp.bfloat16), 'pipe', scatter_dimensi...  10.4 us
  transfers between devices with their start and end apart: 21, of which 15 were waited for; matrix products, arithmetic and copies ran while one was open for 17% of the time, Pallas kernels for 0%

profile of v1, /device:TPU:0, one launch (start us, length us, event | category | flops | bytes accessed | tf_op | source)
XLA Modules:
  0.0 326.7 jit_solution(11520756220992197344)
XLA Ops:
  8.6 3.4 %scatter_custom_fusion = s32[1024]{0:T(1024)S(1)} fusion(s32[768]{0:T(1024)S(1)} %fusion.23, s32[768]{0:T(1024)S(1)} %add_select_fusion, s32[]{:T(128)} %constant.138.clone.1), kind=kCustom, calls=%fused_computation.96 | custom fusion | bytes 4100 | tf_op jit(solution)/shard_map/scatter | solution.py:92
  12.0 1.0 constant_dynamic-slice_fusion
  13.0 4.0 %gather_fusion.3 = bf16[1024,512]{1,0:T(8,128)(2,1)S(1)} fusion(bf16[128,512]{1,0:T(8,128)(2,1)S(1)} %get-tuple-element.31, s32[1024]{0:T(1024)S(1)} %fusion.22), kind=kCustom, calls=%fused_computation.2.clone | custom fusion | bytes 2101248 | tf_op jit(solution)/shard_map/jit(_take)/gather | solution.py:103
  17.0 5.1 %gather_fusion.1 = bf16[1024,512]{1,0:T(8,128)(2,1)} fusion(bf16[128,512]{1,0:T(8,128)(2,1)S(1)} %get-tuple-element.32, s32[1024]{0:T(1024)S(1)} %fusion.22), kind=kCustom, calls=%fused_computation.clone | custom fusion | bytes 2101248 | tf_op jit(solution)/shard_map/jit(_take)/gather | solution.py:103
  22.1 2.4 broadcast_select_fusion.2
  24.6 5.5 %collective-permute-start.14 = (bf16[1,64,512]{2,1,0:T(8,128)(2,1)S(1)}, bf16[1,64,512]{2,1,0:T(8,128)(2,1)S(1)}, u32[]{:S(2)}, u32[]{:S(2)}) collective-permute-start(bf16[1,64,512]{2,1,0:T(8,128)(2,1)S(1)} %get-tuple-element.11), channel_id=1, source_target_pairs={{0,15},{1,0},{2,1},{3,2},{4,3},{5,4},{6,5},{7,6},{8,7},{9,8},{10,9... | collective-permute-start | bytes 196616 | tf_op jit(solution)/shard_map/ppermute | solution.py:28
  32.3 5.5 %collective-permute-done = bf16[1,64,512]{2,1,0:T(8,128)(2,1)S(1)} collective-permute-done((bf16[1,64,512]{2,1,0:T(8,128)(2,1)S(1)}, bf16[1,64,512]{2,1,0:T(8,128)(2,1)S(1)}, u32[]{:S(2)}, u32[]{:S(2)}) %collective-permute-start) | collective-permute-done | bytes 65568 | tf_op jit(solution)/shard_map/ppermute | solution.py:28
  37.8 7.0 %collective-permute-done.1 = bf16[1,64,512]{2,1,0:T(8,128)(2,1)S(1)} collective-permute-done((bf16[1,64,512]{2,1,0:T(8,128)(2,1)S(1)}, bf16[1,64,512]{2,1,0:T(8,128)(2,1)S(1)}, u32[]{:S(2)}, u32[]{:S(2)}) %collective-permute-start.1) | collective-permute-done | bytes 65568 | tf_op jit(solution)/shard_map/ppermute | solution.py:28
  44.8 5.5 %collective-permute-done.2 = bf16[1,64,512]{2,1,0:T(8,128)(2,1)S(1)} collective-permute-done((bf16[1,64,512]{2,1,0:T(8,128)(2,1)S(1)}, bf16[1,64,512]{2,1,0:T(8,128)(2,1)S(1)}, u32[]{:S(2)}, u32[]{:S(2)}) %collective-permute-start.2) | collective-permute-done | bytes 65568 | tf_op jit(solution)/shard_map/ppermute | solution.py:28
  50.3 6.1 %collective-permute-done.3 = bf16[1,64,512]{2,1,0:T(8,128)(2,1)S(1)} collective-permute-done((bf16[1,64,512]{2,1,0:T(8,128)(2,1)S(1)}, bf16[1,64,512]{2,1,0:T(8,128)(2,1)S(1)}, u32[]{:S(2)}, u32[]{:S(2)}) %collective-permute-start.3) | collective-permute-done | bytes 65568 | tf_op jit(solution)/shard_map/ppermute | solution.py:28
  56.3 5.5 %collective-permute-done.4 = bf16[1,64,512]{2,1,0:T(8,128)(2,1)S(1)} collective-permute-done((bf16[1,64,512]{2,1,0:T(8,128)(2,1)S(1)}, bf16[1,64,512]{2,1,0:T(8,128)(2,1)S(1)}, u32[]{:S(2)}, u32[]{:S(2)}) %collective-permute-start.4) | collective-permute-done | bytes 65568 | tf_op jit(solution)/shard_map/ppermute | solution.py:28
  61.8 6.1 %collective-permute-done.5 = bf16[1,64,512]{2,1,0:T(8,128)(2,1)S(1)} collective-permute-done((bf16[1,64,512]{2,1,0:T(8,128)(2,1)S(1)}, bf16[1,64,512]{2,1,0:T(8,128)(2,1)S(1)}, u32[]{:S(2)}, u32[]{:S(2)}) %collective-permute-start.5) | collective-permute-done | bytes 65568 | tf_op jit(solution)/shard_map/ppermute | solution.py:28
  67.9 4.6 %collective-permute-done.6 = bf16[1,64,512]{2,1,0:T(8,128)(2,1)S(1)} collective-permute-done((bf16[1,64,512]{2,1,0:T(8,128)(2,1)S(1)}, bf16[1,64,512]{2,1,0:T(8,128)(2,1)S(1)}, u32[]{:S(2)}, u32[]{:S(2)}) %collective-permute-start.6) | collective-permute-done | bytes 65568 | tf_op jit(solution)/shard_map/ppermute | solution.py:28
  72.5 5.2 %collective-permute-done.7 = bf16[1,64,512]{2,1,0:T(8,128)(2,1)S(1)} collective-permute-done((bf16[1,64,512]{2,1,0:T(8,128)(2,1)S(1)}, bf16[1,64,512]{2,1,0:T(8,128)(2,1)S(1)}, u32[]{:S(2)}, u32[]{:S(2)}) %collective-permute-start.7) | collective-permute-done | bytes 65568 | tf_op jit(solution)/shard_map/ppermute | solution.py:28
  77.6 4.6 %collective-permute-done.8 = bf16[1,64,512]{2,1,0:T(8,128)(2,1)S(1)} collective-permute-done((bf16[1,64,512]{2,1,0:T(8,128)(2,1)S(1)}, bf16[1,64,512]{2,1,0:T(8,128)(2,1)S(1)}, u32[]{:S(2)}, u32[]{:S(2)}) %collective-permute-start.8) | collective-permute-done | bytes 65568 | tf_op jit(solution)/shard_map/ppermute | solution.py:28
  82.2 1.8 collective-permute-start.9
  84.0 3.3 %collective-permute-done.9 = bf16[1,64,512]{2,1,0:T(8,128)(2,1)S(1)} collective-permute-done((bf16[1,64,512]{2,1,0:T(8,128)(2,1)S(1)}, bf16[1,64,512]{2,1,0:T(8,128)(2,1)S(1)}, u32[]{:S(2)}, u32[]{:S(2)}) %collective-permute-start.9) | collective-permute-done | bytes 65568 | tf_op jit(solution)/shard_map/ppermute | solution.py:28
  88.3 2.8 collective-permute-done.10
  91.2 1.6 gather_fusion
  92.8 32.7 %all_to_all.25 = bf16[16,64,512]{2,1,0:T(8,128)(2,1)} all-to-all(bf16[16,64,512]{2,1,0:T(8,128)(2,1)S(1)} %bitcast.127), channel_id=1, replica_groups=mesh['pipe'=2,'expert'=16] {'expert'}, dimensions={0} | all-to-all | bytes 2097152 | tf_op jit(solution)/shard_map/all_to_all | solution.py:110
  125.9 8.6 %scatter_custom_fusion.1 = bf16[1024]{0:T(1024)(128)(2,1)S(1)} fusion(s32[768]{0:T(1024)S(1)} %fusion.23, bf16[768]{0:T(1024)(128)(2,1)S(1)} %reshape.228, bf16[]{:T(256)} %constant.160.clone.1), kind=kCustom, calls=%fused_computation.99 | custom fusion | bytes 2050 | tf_op jit(solution)/shard_map/scatter | solution.py:96
  134.6 11.2 %all_to_all.26 = bf16[16,1,64]{2,1,0:T(2,128)(2,1)S(1)} all-to-all(bf16[16,1,64]{2,1,0:T(2,128)(2,1)S(1)} %all_to_all.20), channel_id=1, replica_groups=mesh['pipe'=2,'expert'=16] {'expert'}, dimensions={0} | all-to-all | bytes 4096 | tf_op jit(solution)/shard_map/all_to_all | solution.py:111
  145.9 5.4 %fusion.9 = f32[1024,704]{0,1:T(8,128)} fusion(bf16[1024,1024]{1,0:T(8,128)(2,1)} %bitcast.139, bf16[1,704,1024]{2,1,0:T(8,128)(2,1)} %param.18), kind=kOutput, calls=%fused_computation.29 | convolution fusion | flops 1476395008 | bytes 6422528 | tf_op jit(solution)/shard_map/dot_general | solution.py:43
  151.4 3.3 %fusion.13 = f32[1024,704]{0,1:T(8,128)} fusion(bf16[1024,1024]{1,0:T(8,128)(2,1)S(1)} %bitcast.141, bf16[1,704,1024]{2,1,0:T(8,128)(2,1)S(1)} %copy-done.9), kind=kOutput, calls=%fused_computation.33 | convolution fusion | flops 1476395008 | bytes 6422528 | tf_op jit(solution)/shard_map/dot_general | solution.py:42
  154.6 9.5 %all-gather.4.cloned.1.call-done = bf16[16,64,1024]{2,1,0:T(8,128)(2,1)} async-done(((bf16[16,64,512]{2,1,0:T(8,128)(2,1)}), bf16[16,64,1024]{2,1,0:T(8,128)(2,1)}) %all-gather.4.cloned.1.call-update) | async-done | bytes 2097168 | tf_op jit(solution)/shard_map/all_gather | solution.py:115
  164.2 2.1 multiply_convert_fusion
  166.6 5.4 %multiply_convert_fusion.1 = (bf16[1024,704]{0,1:T(8,128)(2,1)}, bf16[1024,704]{0,1:T(8,128)(2,1)}, bf16[1024,704]{0,1:T(8,128)(2,1)S(1)}) fusion(f32[1024,704]{0,1:T(8,128)} %fusion.13, f32[1024,704]{0,1:T(8,128)S(1)} %copy-done.11, bf16[1024,1024]{1,0:T(8,128)(2,1)S(1)} %bitcast.131, bf16[1,704,1024]{2,1,0:T(8,128)(2,1)S(1)} %copy-done), kind=kOutput, calls=%fused_computation.11 | convolution fusion | flops 1487208448 | bytes 13631488 | tf_op jit(solution)/shard_map/dot_general | solution.py:58
  172.0 3.2 convolution_convert_fusion
  175.2 5.6 %all-to-all-start = ((bf16[16,64,1024]{2,1,0:T(8,128)(2,1)}), bf16[16,64,1024]{2,1,0:T(8,128)(2,1)S(1)}, u32[]{:S(2)}, u32[]{:S(2)}) async-start(bf16[16,64,1024]{2,1,0:T(8,128)(2,1)} %bitcast.130), calls=%async_computation | async-start | bytes 4194304 | tf_op jit(solution)/shard_map/all_to_all | solution.py:129
  180.9 3.8 %fusion.11 = f32[1024,1024]{1,0:T(8,128)S(1)} fusion(bf16[1024,704]{0,1:T(8,128)(2,1)} %get-tuple-element.9, bf16[1,704,1024]{2,1,0:T(8,128)(2,1)} %param.17), kind=kOutput, calls=%fused_computation.31 | convolution fusion | flops 1476395008 | bytes 7077888 | tf_op jit(solution)/shard_map/dot_general | solution.py:62
  184.7 3.3 %add_convert_fusion = bf16[1024,1024]{1,0:T(8,128)(2,1)} fusion(f32[1024,1024]{1,0:T(8,128)S(1)} %fusion.11, bf16[1024,704]{0,1:T(8,128)(2,1)S(1)} %copy-done.13, bf16[1,704,1024]{2,1,0:T(8,128)(2,1)S(1)} %copy-done.10), kind=kOutput, calls=%fused_computation.9 | convolution fusion | flops 1478492160 | bytes 9175040 | tf_op jit(solution)/shard_map/dot_general | solution.py:63
  188.0 33.8 %all-to-all-done = bf16[16,64,1024]{2,1,0:T(8,128)(2,1)S(1)} async-done(((bf16[16,64,1024]{2,1,0:T(8,128)(2,1)}), bf16[16,64,1024]{2,1,0:T(8,128)(2,1)S(1)}, u32[]{:S(2)}, u32[]{:S(2)}) %all-to-all-start) | async-done | bytes 2097184 | tf_op jit(solution)/shard_map/all_to_all | solution.py:129
  221.8 11.3 %all-to-all-start.3 = ((bf16[16,64,1024]{2,1,0:T(8,128)(2,1)}), bf16[16,64,1024]{2,1,0:T(8,128)(2,1)}, u32[]{:S(2)}, u32[]{:S(2)}) async-start(bf16[16,64,1024]{2,1,0:T(8,128)(2,1)} %bitcast.129), calls=%async_computation.4 | async-start | bytes 4194304 | tf_op jit(solution)/shard_map/all_to_all | solution.py:145
  233.4 1.0 reshape.164
  237.1 4.9 %fusion.3 = bf16[1,704,1024]{2,1,0:T(8,128)(2,1)} fusion(bf16[1024,704]{0,1:T(8,128)(2,1)} %get-tuple-element.8, bf16[1024,1024]{1,0:T(8,128)(2,1)} %bitcast.140), kind=kOutput, calls=%fused_computation.23 | convolution fusion | flops 1477115904 | bytes 4980736 | tf_op jit(solution)/shard_map/dot_general | solution.py:68
  242.0 2.8 fusion.2
  244.8 3.6 %gather_fusion.2 = bf16[768,1024]{1,0:T(8,128)(2,1)} fusion(bf16[1024,1024]{1,0:T(8,128)(2,1)S(1)} %bitcast.126, s32[1024]{0:T(1024)S(1)} %pad_clamp_fusion), kind=kCustom, calls=%fused_computation.1.clone | custom fusion | bytes 3148800 | tf_op jit(solution)/shard_map/jit(_take)/gather | solution.py:80
  248.4 25.8 %all-to-all-done.3 = bf16[16,64,1024]{2,1,0:T(8,128)(2,1)} async-done(((bf16[16,64,1024]{2,1,0:T(8,128)(2,1)}), bf16[16,64,1024]{2,1,0:T(8,128)(2,1)}, u32[]{:S(2)}, u32[]{:S(2)}) %all-to-all-start.3) | async-done | bytes 2097184 | tf_op jit(solution)/shard_map/all_to_all | solution.py:145
  274.1 6.5 %gather_fusion.4 = bf16[768,1024]{1,0:T(8,128)(2,1)} fusion(bf16[1024,1024]{1,0:T(8,128)(2,1)} %bitcast.45, s32[1024]{0:T(1024)S(1)} %pad_clamp_fusion), kind=kCustom, calls=%fused_computation.3.clone | custom fusion | bytes 3148800 | tf_op jit(solution)/shard_map/jit(_take)/gather | solution.py:80
  280.7 3.5 %broadcast_select_fusion = (bf16[768,1024]{1,0:T(8,128)(2,1)}, bf16[768,1024]{1,0:T(8,128)(2,1)}) fusion(bf16[768,1024]{1,0:T(8,128)(2,1)} %gather_fusion.4, pred[768]{0:T(1024)(128)(4,1)S(1)} %copy-done.6, bf16[768,1024]{1,0:T(8,128)(2,1)S(1)} %copy-done.1), kind=kLoop, calls=%fused_computation.20 | loop fusion | flops 1572864 | bytes 6292224 | tf_op jit(solution)/shard_map/jit(_take)/select_n | solution.py:80
  284.2 2.5 reshape.170
  288.2 3.4 %fusion = bf16[1024,1024]{1,0:T(8,128)(2,1)} fusion(f32[1024]{0:T(1024)S(1)} %reshape.172, bf16[16,64,1024]{2,1,0:T(8,128)(2,1)} %all-gather.4.cloned.1.call-done), kind=kLoop, calls=%fused_computation.8 | loop fusion | flops 3145728 | bytes 4198400 | tf_op jit(solution)/shard_map/convert_element_type | solution.py:55
  291.6 2.5 reshape.165
  294.0 1.5 fusion.31
  296.4 4.8 %fusion.4 = bf16[1,704,1024]{2,1,0:T(8,128)(2,1)} fusion(bf16[1024,704]{0,1:T(8,128)(2,1)} %copy-done.14, bf16[1024,1024]{1,0:T(8,128)(2,1)} %fusion), kind=kOutput, calls=%fused_computation.24 | convolution fusion | flops 1477115904 | bytes 4980736 | tf_op jit(solution)/shard_map/dot_general | solution.py:71
  301.2 2.1 fusion.15
  304.2 5.6 %psum.7 = f32[128,6]{0,1:T(8,128)} all-reduce(f32[128,6]{0,1:T(8,128)S(1)} %bitcast.137), channel_id=1, replica_groups=mesh['pipe'=2,'expert'=16] {'pipe'}, use_global_device_ids=true, to_apply=%region_4.7 | all-reduce | flops 768 | bytes 6144 | tf_op jit(solution)/shard_map/psum | solution.py:159
  309.7 10.4 %reduce-scatter.3.cloned.1.call-done = bf16[128,512]{1,0:T(8,128)(2,1)} async-done(((bf16[128,1024]{1,0:T(8,128)(2,1)}), bf16[128,512]{1,0:T(8,128)(2,1)}) %reduce-scatter.3.cloned.1.call-update) | async-done | bytes 131088 | tf_op jit(solution)/shard_map/reduce_scatter | solution.py:139
  (96 shorter events, 11.6 us)
Async XLA Ops:
  7.2 159.1 %copy-start = (bf16[1,704,1024]{2,1,0:T(8,128)(2,1)S(1)}, bf16[1,704,1024]{2,1,0:T(8,128)(2,1)}, u32[]{:S(2)}) copy-start(bf16[1,704,1024]{2,1,0:T(8,128)(2,1)} %param.19) | copy-start | bytes 4325380
  7.2 138.7 %all-gather.6.cloned.1.call-start = ((), (), s32[]{:S(2)}) async-start(), calls=%async_computation.9 | async-start | bytes 3145728 | tf_op jit(solution)/shard_map/all_gather | solution.py:114
  8.4 3.6 %copy-start.3 = (s32[128,6]{1,0:T(8,128)}, s32[128,6]{1,0:T(8,128)S(1)}, u32[]{:S(2)}) copy-start(s32[128,6]{1,0:T(8,128)S(1)} %copy.20) | copy-start | bytes 9220
  24.6 66.6 %collective-permute-start.14 = (bf16[1,64,512]{2,1,0:T(8,128)(2,1)S(1)}, bf16[1,64,512]{2,1,0:T(8,128)(2,1)S(1)}, u32[]{:S(2)}, u32[]{:S(2)}) collective-permute-start(bf16[1,64,512]{2,1,0:T(8,128)(2,1)S(1)} %get-tuple-element.11), channel_id=1, source_target_pairs={{0,15},{1,0},{2,1},{3,2},{4,3},{5,4},{6,5},{7,6},{8,7},{9,8},{10,9... | collective-permute-start | bytes 196616 | tf_op jit(solution)/shard_map/ppermute | solution.py:28
  30.1 61.0 %collective-permute-start.13 = (bf16[1,64,512]{2,1,0:T(8,128)(2,1)S(1)}, bf16[1,64,512]{2,1,0:T(8,128)(2,1)S(1)}, u32[]{:S(2)}, u32[]{:S(2)}) collective-permute-start(bf16[1,64,512]{2,1,0:T(8,128)(2,1)S(1)} %get-tuple-element.12), channel_id=1, source_target_pairs={{0,14},{1,15},{2,0},{3,1},{4,2},{5,3},{6,4},{7,5},{8,6},{9,7},{10,... | collective-permute-start | bytes 196616 | tf_op jit(solution)/shard_map/ppermute | solution.py:28
  30.7 60.4 %collective-permute-start.12 = (bf16[1,64,512]{2,1,0:T(8,128)(2,1)S(1)}, bf16[1,64,512]{2,1,0:T(8,128)(2,1)S(1)}, u32[]{:S(2)}, u32[]{:S(2)}) collective-permute-start(bf16[1,64,512]{2,1,0:T(8,128)(2,1)S(1)} %get-tuple-element.13), channel_id=1, source_target_pairs={{0,13},{1,14},{2,15},{3,0},{4,1},{5,2},{6,3},{7,4},{8,5},{9,6},{10... | collective-permute-start | bytes 196616 | tf_op jit(solution)/shard_map/ppermute | solution.py:28
  31.0 60.1 %collective-permute-start.11 = (bf16[1,64,512]{2,1,0:T(8,128)(2,1)S(1)}, bf16[1,64,512]{2,1,0:T(8,128)(2,1)S(1)}, u32[]{:S(2)}, u32[]{:S(2)}) collective-permute-start(bf16[1,64,512]{2,1,0:T(8,128)(2,1)S(1)} %get-tuple-element.14), channel_id=1, source_target_pairs={{0,12},{1,13},{2,14},{3,15},{4,0},{5,1},{6,2},{7,3},{8,4},{9,5},{1... | collective-permute-start | bytes 196616 | tf_op jit(solution)/shard_map/ppermute | solution.py:28
  31.4 6.4 %collective-permute-start = (bf16[1,64,512]{2,1,0:T(8,128)(2,1)S(1)}, bf16[1,64,512]{2,1,0:T(8,128)(2,1)S(1)}, u32[]{:S(2)}, u32[]{:S(2)}) collective-permute-start(bf16[1,64,512]{2,1,0:T(8,128)(2,1)S(1)} %get-tuple-element.25), channel_id=1, source_target_pairs={{0,1},{1,2},{2,3},{3,4},{4,5},{5,6},{6,7},{7,8},{8,9},{9,10},{10,1... | collective-permute-start | bytes 196616 | tf_op jit(solution)/shard_map/ppermute | solution.py:28
  37.8 7.0 %collective-permute-start.1 = (bf16[1,64,512]{2,1,0:T(8,128)(2,1)S(1)}, bf16[1,64,512]{2,1,0:T(8,128)(2,1)S(1)}, u32[]{:S(2)}, u32[]{:S(2)}) collective-permute-start(bf16[1,64,512]{2,1,0:T(8,128)(2,1)S(1)} %get-tuple-element.24), channel_id=1, source_target_pairs={{0,2},{1,3},{2,4},{3,5},{4,6},{5,7},{6,8},{7,9},{8,10},{9,11},{10,... | collective-permute-start | bytes 196616 | tf_op jit(solution)/shard_map/ppermute | solution.py:28
  44.8 5.5 %collective-permute-start.2 = (bf16[1,64,512]{2,1,0:T(8,128)(2,1)S(1)}, bf16[1,64,512]{2,1,0:T(8,128)(2,1)S(1)}, u32[]{:S(2)}, u32[]{:S(2)}) collective-permute-start(bf16[1,64,512]{2,1,0:T(8,128)(2,1)S(1)} %get-tuple-element.23), channel_id=1, source_target_pairs={{0,3},{1,4},{2,5},{3,6},{4,7},{5,8},{6,9},{7,10},{8,11},{9,12},{10... | collective-permute-start | bytes 196616 | tf_op jit(solution)/shard_map/ppermute | solution.py:28
  50.2 6.1 %collective-permute-start.3 = (bf16[1,64,512]{2,1,0:T(8,128)(2,1)S(1)}, bf16[1,64,512]{2,1,0:T(8,128)(2,1)S(1)}, u32[]{:S(2)}, u32[]{:S(2)}) collective-permute-start(bf16[1,64,512]{2,1,0:T(8,128)(2,1)S(1)} %get-tuple-element.22), channel_id=1, source_target_pairs={{0,4},{1,5},{2,6},{3,7},{4,8},{5,9},{6,10},{7,11},{8,12},{9,13},{1... | collective-permute-start | bytes 196616 | tf_op jit(solution)/shard_map/ppermute | solution.py:28
  56.3 5.5 %collective-permute-start.4 = (bf16[1,64,512]{2,1,0:T(8,128)(2,1)S(1)}, bf16[1,64,512]{2,1,0:T(8,128)(2,1)S(1)}, u32[]{:S(2)}, u32[]{:S(2)}) collective-permute-start(bf16[1,64,512]{2,1,0:T(8,128)(2,1)S(1)} %get-tuple-element.21), channel_id=1, source_target_pairs={{0,5},{1,6},{2,7},{3,8},{4,9},{5,10},{6,11},{7,12},{8,13},{9,14},{... | collective-permute-start | bytes 196616 | tf_op jit(solution)/shard_map/ppermute | solution.py:28
  61.8 6.1 %collective-permute-start.5 = (bf16[1,64,512]{2,1,0:T(8,128)(2,1)S(1)}, bf16[1,64,512]{2,1,0:T(8,128)(2,1)S(1)}, u32[]{:S(2)}, u32[]{:S(2)}) collective-permute-start(bf16[1,64,512]{2,1,0:T(8,128)(2,1)S(1)} %get-tuple-element.20), channel_id=1, source_target_pairs={{0,6},{1,7},{2,8},{3,9},{4,10},{5,11},{6,12},{7,13},{8,14},{9,15},... | collective-permute-start | bytes 196616 | tf_op jit(solution)/shard_map/ppermute | solution.py:28
  67.9 4.6 %collective-permute-start.6 = (bf16[1,64,512]{2,1,0:T(8,128)(2,1)S(1)}, bf16[1,64,512]{2,1,0:T(8,128)(2,1)S(1)}, u32[]{:S(2)}, u32[]{:S(2)}) collective-permute-start(bf16[1,64,512]{2,1,0:T(8,128)(2,1)S(1)} %get-tuple-element.19), channel_id=1, source_target_pairs={{0,7},{1,8},{2,9},{3,10},{4,11},{5,12},{6,13},{7,14},{8,15},{9,0},... | collective-permute-start | bytes 196616 | tf_op jit(solution)/shard_map/ppermute | solution.py:28
  72.5 5.2 %collective-permute-start.7 = (bf16[1,64,512]{2,1,0:T(8,128)(2,1)S(1)}, bf16[1,64,512]{2,1,0:T(8,128)(2,1)S(1)}, u32[]{:S(2)}, u32[]{:S(2)}) collective-permute-start(bf16[1,64,512]{2,1,0:T(8,128)(2,1)S(1)} %get-tuple-element.18), channel_id=1, source_target_pairs={{0,8},{1,9},{2,10},{3,11},{4,12},{5,13},{6,14},{7,15},{8,0},{9,1},... | collective-permute-start | bytes 196616 | tf_op jit(solution)/shard_map/ppermute | solution.py:28
  77.6 15.2 %copy-start.2 = (bf16[1024,512]{1,0:T(8,128)(2,1)S(1)}, bf16[1024,512]{1,0:T(8,128)(2,1)}, u32[]{:S(2)}) copy-start(bf16[1024,512]{1,0:T(8,128)(2,1)} %get-tuple-element.29) | copy-start | bytes 3145732
  77.6 4.6 %collective-permute-start.8 = (bf16[1,64,512]{2,1,0:T(8,128)(2,1)S(1)}, bf16[1,64,512]{2,1,0:T(8,128)(2,1)S(1)}, u32[]{:S(2)}, u32[]{:S(2)}) collective-permute-start(bf16[1,64,512]{2,1,0:T(8,128)(2,1)S(1)} %get-tuple-element.17), channel_id=1, source_target_pairs={{0,9},{1,10},{2,11},{3,12},{4,13},{5,14},{6,15},{7,0},{8,1},{9,2},... | collective-permute-start | bytes 196616 | tf_op jit(solution)/shard_map/ppermute | solution.py:28
  82.2 5.2 %collective-permute-start.9 = (bf16[1,64,512]{2,1,0:T(8,128)(2,1)S(1)}, bf16[1,64,512]{2,1,0:T(8,128)(2,1)S(1)}, u32[]{:S(2)}, u32[]{:S(2)}) collective-permute-start(bf16[1,64,512]{2,1,0:T(8,128)(2,1)S(1)} %get-tuple-element.16), channel_id=1, source_target_pairs={{0,10},{1,11},{2,12},{3,13},{4,14},{5,15},{6,0},{7,1},{8,2},{9,3},... | collective-permute-start | bytes 196616 | tf_op jit(solution)/shard_map/ppermute | solution.py:28
  87.4 3.7 %collective-permute-start.10 = (bf16[1,64,512]{2,1,0:T(8,128)(2,1)S(1)}, bf16[1,64,512]{2,1,0:T(8,128)(2,1)S(1)}, u32[]{:S(2)}, u32[]{:S(2)}) collective-permute-start(bf16[1,64,512]{2,1,0:T(8,128)(2,1)S(1)} %get-tuple-element.15), channel_id=1, source_target_pairs={{0,11},{1,12},{2,13},{3,14},{4,15},{5,0},{6,1},{7,2},{8,3},{9,4},{... | collective-permute-start | bytes 196616 | tf_op jit(solution)/shard_map/ppermute | solution.py:28
  92.8 32.8 %copy-start.5 = (bf16[128,6]{0,1:T(8,128)(2,1)S(1)}, bf16[128,6]{0,1:T(8,128)(2,1)}, u32[]{:S(2)}) copy-start(bf16[128,6]{0,1:T(8,128)(2,1)} %param.16) | copy-start | bytes 4612
  92.8 71.4 %all-gather.4.cloned.1.call-start = ((), (), s32[]{:S(2)}) async-start(), calls=%async_computation.7 | async-start | bytes 3145728 | tf_op jit(solution)/shard_map/all_gather | solution.py:115
  145.9 5.5 %copy-start.7 = (bf16[16,64,1024]{2,1,0:T(8,128)(2,1)S(1)}, bf16[16,64,1024]{2,1,0:T(8,128)(2,1)}, u32[]{:S(2)}) copy-start(bf16[16,64,1024]{2,1,0:T(8,128)(2,1)} %all-gather.6.cloned.1.call-done) | copy-start | bytes 6291460
  145.9 5.5 %copy-start.9 = (bf16[1,704,1024]{2,1,0:T(8,128)(2,1)S(1)}, bf16[1,704,1024]{2,1,0:T(8,128)(2,1)}, u32[]{:S(2)}) copy-start(bf16[1,704,1024]{2,1,0:T(8,128)(2,1)} %param.17) | copy-start | bytes 4325380
  164.2 2.4 copy-start.11
  172.0 3.2 copy-start.14
  175.2 46.6 %all-to-all-start = ((bf16[16,64,1024]{2,1,0:T(8,128)(2,1)}), bf16[16,64,1024]{2,1,0:T(8,128)(2,1)S(1)}, u32[]{:S(2)}, u32[]{:S(2)}) async-start(bf16[16,64,1024]{2,1,0:T(8,128)(2,1)} %bitcast.130), calls=%async_computation | async-start | bytes 4194304 | tf_op jit(solution)/shard_map/all_to_all | solution.py:129
  180.9 3.8 %copy-start.10 = (bf16[1,704,1024]{2,1,0:T(8,128)(2,1)S(1)}, bf16[1,704,1024]{2,1,0:T(8,128)(2,1)}, u32[]{:S(2)}) copy-start(bf16[1,704,1024]{2,1,0:T(8,128)(2,1)} %param.18) | copy-start | bytes 4325380
  180.9 3.8 %copy-start.13 = (bf16[1024,704]{0,1:T(8,128)(2,1)S(1)}, bf16[1024,704]{0,1:T(8,128)(2,1)}, u32[]{:S(2)}) copy-start(bf16[1024,704]{0,1:T(8,128)(2,1)} %get-tuple-element.8) | copy-start | bytes 4325380
  221.8 52.3 %all-to-all-start.3 = ((bf16[16,64,1024]{2,1,0:T(8,128)(2,1)}), bf16[16,64,1024]{2,1,0:T(8,128)(2,1)}, u32[]{:S(2)}, u32[]{:S(2)}) async-start(bf16[16,64,1024]{2,1,0:T(8,128)(2,1)} %bitcast.129), calls=%async_computation.4 | async-start | bytes 4194304 | tf_op jit(solution)/shard_map/all_to_all | solution.py:145
  233.1 76.6 %reduce-scatter.5.cloned.1.call-start = ((), (), s32[]{:S(2)}) async-start(), calls=%async_computation.8 | async-start | bytes 393216 | tf_op jit(solution)/shard_map/reduce_scatter | solution.py:156
  237.1 4.9 %copy-start.8 = (bf16[16,64,1024]{2,1,0:T(8,128)(2,1)S(1)}, bf16[16,64,1024]{2,1,0:T(8,128)(2,1)}, u32[]{:S(2)}) copy-start(bf16[16,64,1024]{2,1,0:T(8,128)(2,1)} %all-gather.6.cloned.1.call-done) | copy-start | bytes 6291460
  237.1 4.9 %copy-start.12 = (bf16[1024,704]{0,1:T(8,128)(2,1)S(1)}, bf16[1024,704]{0,1:T(8,128)(2,1)}, u32[]{:S(2)}) copy-start(bf16[1024,704]{0,1:T(8,128)(2,1)} %get-tuple-element.9) | copy-start | bytes 4325380
  274.1 6.5 %copy-start.1 = (bf16[768,1024]{1,0:T(8,128)(2,1)S(1)}, bf16[768,1024]{1,0:T(8,128)(2,1)}, u32[]{:S(2)}) copy-start(bf16[768,1024]{1,0:T(8,128)(2,1)} %gather_fusion.2) | copy-start | bytes 4718596
  274.1 6.5 %copy-start.6 = (pred[768]{0:T(1024)(128)(4,1)S(1)}, pred[768]{0:T(1024)(128)(4,1)}, u32[]{:S(2)}) copy-start(pred[768]{0:T(1024)(128)(4,1)} %compare_and_fusion) | copy-start | bytes 2308
  288.1 32.0 %reduce-scatter.3.cloned.1.call-start = ((), (), s32[]{:S(2)}) async-start(), calls=%async_computation.6 | async-start | bytes 393216 | tf_op jit(solution)/shard_map/reduce_scatter | solution.py:139
  296.4 4.8 %copy-start.4 = (bf16[128,1024]{1,0:T(8,128)(2,1)S(1)}, bf16[128,1024]{1,0:T(8,128)(2,1)}, u32[]{:S(2)}) copy-start(bf16[128,1024]{1,0:T(8,128)(2,1)} %param.13) | copy-start | bytes 786436
Sparse Core Ops, SparseCore 0:
  92.9 36.5 all-gather.5
  131.0 33.0 all-gather.3
  288.3 17.3 reduce-scatter.4
  308.4 11.7 reduce-scatter.2
